TPU v7x, 256 devices: a whole 4x4x8 slice. The times are simulated.
256 devices in a mesh: row: 16 (over z, core), col: 16 (over y, x).
Axes of the slice: x: 4, y: 4, z: 8, core: 2. Of those that a mesh axis runs over, the one named last changes fastest.
Arguments:
- points: float32 [32, 65536], P(None, ('row', 'col')), may hold values from -6 to 6
- search: float32 [96, 65536], P(None, ('row', 'col')), may hold values from -24 to 24
Outputs:
- applied: float32 [96, 65536], P(None, ('row', 'col'))
- gram_a: float32 [96, 96], replicated
- gram_b: float32 [96, 96], replicated
- q_block: float32 [32, 65536], P(None, ('row', 'col'))
All inputs are finite; a program needn't handle non-finite values.
Results may differ from a plain program's by a relative error of at most 0.00036.
Values may be sent and summed in bfloat16 or wider, within the bound.
A program may use at most 128 MiB of HBM per device.

v0:
```python
import jax
import jax.numpy as jnp
from jax import lax
from jax.sharding import PartitionSpec as P

NEV = 32


def step_width():
    return 256


def pair_tile(source_points, source_squares, target_points, target_squares, kernel_rate):
    cross_terms = lax.dot_general(
        source_points,
        target_points,
        (((0,), (0,)), ((), ())),
        precision=lax.Precision.HIGHEST,
        preferred_element_type=jnp.float32,
    )
    return jnp.exp(
        -kernel_rate * (source_squares[:, None] + target_squares[None, :] - 2.0 * cross_terms)
    )


def degree_stored(source_points, source_squares, target_points, target_squares, kernel_rate):
    span_width = source_points.shape[1]
    stride = step_width()

    def degree_add_block(step_index, carry):
        running, stored = carry
        offset = step_index * stride
        block_points = lax.dynamic_slice_in_dim(source_points, offset, stride, 1)
        block_squares = lax.dynamic_slice_in_dim(source_squares, offset, stride, 0)
        affinity = pair_tile(
            block_points, block_squares, target_points, target_squares, kernel_rate
        )
        stored = lax.dynamic_update_slice_in_dim(stored, affinity.astype(jnp.bfloat16), offset, 0)
        return (running + jnp.sum(affinity, axis=0), stored)

    zero_sums = jnp.zeros((target_points.shape[1],), jnp.float32)
    empty_tile = jnp.zeros((span_width, target_points.shape[1]), jnp.bfloat16)
    return lax.fori_loop(0, span_width // stride, degree_add_block, (zero_sums, empty_tile))


def fold_stored(stored):

    def accumulate(running, shard_piece, first_index):
        span_width = shard_piece.shape[1]
        stride = step_width()

        def accumulate_add_block(step_index, partial_value):
            offset = step_index * stride
            columns = lax.dynamic_slice_in_dim(shard_piece, offset, stride, 1)
            tile_rows = lax.dynamic_slice_in_dim(stored, offset, stride, 0)
            return partial_value + jnp.dot(columns, tile_rows, preferred_element_type=jnp.float32)

        return lax.fori_loop(0, span_width // stride, accumulate_add_block, running)

    return accumulate


def degrees_and_fold(source_points, target_points, kernel_rate):
    target_squares = jnp.sum(target_points * target_points, axis=0)
    source_squares = jnp.sum(source_points * source_points, axis=0)
    partial_value, stored = degree_stored(
        source_points, source_squares, target_points, target_squares, kernel_rate
    )
    accumulate = fold_stored(stored)
    return (partial_value, accumulate)


def per_device(points, search):
    kernel_rate = 2.0 / points.shape[0]
    target_points = lax.all_gather(points, "col", axis=1, tiled=True)
    source_points = lax.all_gather(points, "row", axis=1, tiled=True)
    partial_value, accumulate = degrees_and_fold(source_points, target_points, kernel_rate)
    degrees = lax.psum_scatter(partial_value, "col", scatter_dimension=0, tiled=True)
    inverse_root = lax.rsqrt(degrees)
    scaled = (search * inverse_root[None, :]).astype(jnp.bfloat16)
    zero_sums = jnp.zeros((search.shape[0], target_points.shape[1]), jnp.float32)
    totals = accumulate(zero_sums, lax.all_gather(scaled, "row", axis=1, tiled=True), jnp.int32(0))
    applied = (
        lax.psum_scatter(totals, "col", scatter_dimension=1, tiled=True) * inverse_root[None, :]
    )
    point_count = search.shape[1] * lax.axis_size("row") * lax.axis_size("col")
    contract = (((1,), (1,)), ((), ()))
    local_a = lax.dot_general(
        search,
        applied,
        contract,
        precision=lax.Precision.HIGHEST,
        preferred_element_type=jnp.float32,
    )
    local_b = lax.dot_general(
        search,
        search,
        contract,
        precision=lax.Precision.HIGHEST,
        preferred_element_type=jnp.float32,
    )
    sum_a, sum_b = lax.psum((local_a, local_b), ("row", "col"))
    gram_a = sum_a / point_count
    gram_b = sum_b / point_count
    factor_b = jnp.linalg.cholesky(gram_b[:NEV, :NEV])
    mapping = jax.scipy.linalg.cho_solve((factor_b, True), gram_a[:NEV, :NEV]).T
    residual = applied[:NEV] - jnp.dot(mapping, search[:NEV], precision=lax.Precision.HIGHEST)
    local_r = lax.dot_general(
        residual,
        residual,
        contract,
        precision=lax.Precision.HIGHEST,
        preferred_element_type=jnp.float32,
    )
    residual_gram = lax.psum(local_r, ("row", "col")) / point_count
    factor_r = jnp.linalg.cholesky(residual_gram)
    q_block = jax.scipy.linalg.solve_triangular(factor_r, residual, lower=True)
    return (applied, gram_a, gram_b, q_block)


def solution(mesh):
    placed = (P(None, ("row", "col")), P(None, ("row", "col")))
    return jax.shard_map(
        per_device,
        mesh=mesh,
        in_specs=placed,
        out_specs=(P(None, ("row", "col")), P(), P(), P(None, ("row", "col"))),
        check_vma=False,
    )
```

profile of v0, /device:TPU:1, one launch (start us, length us, event | category | flops | bytes accessed | tf_op | source)
XLA Modules:
  0.0 711.1 jit_solution(5972083221102079643)
XLA Ops:
  7.2 20.0 %all_gather.10 = f32[32,4096]{1,0:T(8,128)S(1)} all-gather(f32[32,256]{1,0:T(8,128)} %param.7), channel_id=1, replica_groups=mesh['row'=16,'col'=16] {'col'}, dimensions={1}, use_global_device_ids=true | all-gather | bytes 557056 | tf_op jit(solution)/shard_map/all_gather | solution.py:75
  27.2 27.3 %all_gather.9 = f32[32,4096]{1,0:T(8,128)S(1)} all-gather(f32[32,256]{1,0:T(8,128)} %param.7), channel_id=1, replica_groups=mesh['row'=16,'col'=16] {'row'}, dimensions={1}, use_global_device_ids=true | all-gather | bytes 557056 | tf_op jit(solution)/shard_map/all_gather | solution.py:76
  54.6 11.0 %broadcast_in_dim.20 = bf16[4096,4096]{1,0:T(8,128)(2,1)} broadcast(bf16[]{:T(256)} %constant.130.clone.1), dimensions={} | broadcast | bytes 33554432 | tf_op jit(solution)/shard_map/broadcast_in_dim | solution.py:42
  65.6 98.8 %while.30 = (s32[]{:T(128)}, f32[4096]{0:T(1024)S(1)}, bf16[4096,4096]{1,0:T(8,128)(2,1)}, f32[4096]{0:T(1024)S(1)}, f32[4096]{0:T(1024)S(1)}, /*index=5*/f32[32...) while((s32[]{:T(128)}, f32[4096]{0:T(1024)S(1)}, ...), condition=%wide.region_4.0_spmd.clone, body=%wide.region_2.0_spmd.clone.sunk | while | flops 408948736 | bytes 6933681 | solution.py:43
  65.6 4.6 fusion.40
  70.3 1.5 convert_dynamic-update-slice_fusion.2
  71.8 4.6 fusion.40
  76.5 1.4 convert_dynamic-update-slice_fusion.2
  78.0 4.6 fusion.40
  82.6 1.5 convert_dynamic-update-slice_fusion.2
  84.1 4.6 fusion.40
  88.7 1.5 convert_dynamic-update-slice_fusion.2
  90.3 4.6 fusion.40
  94.9 1.5 convert_dynamic-update-slice_fusion.2
  96.5 4.6 fusion.40
  101.2 1.4 convert_dynamic-update-slice_fusion.2
  102.7 4.6 fusion.40
  107.3 1.5 convert_dynamic-update-slice_fusion.2
  108.9 4.6 fusion.40
  113.5 1.5 convert_dynamic-update-slice_fusion.2
  115.0 4.6 fusion.40
  119.7 1.5 convert_dynamic-update-slice_fusion.2
  121.2 4.6 fusion.40
  125.8 1.4 convert_dynamic-update-slice_fusion.2
  127.4 4.6 fusion.40
  132.0 1.5 convert_dynamic-update-slice_fusion.2
  133.5 4.6 fusion.40
  138.1 1.5 convert_dynamic-update-slice_fusion.2
  139.7 4.6 fusion.40
  144.3 1.5 convert_dynamic-update-slice_fusion.2
  145.9 4.6 fusion.40
  150.5 1.4 convert_dynamic-update-slice_fusion.2
  152.1 4.6 fusion.40
  156.7 1.5 convert_dynamic-update-slice_fusion.2
  158.3 4.6 fusion.40
  162.9 1.5 convert_dynamic-update-slice_fusion.2
  164.3 58.1 %all-reduce = f32[4096]{0:T(1024)S(1)} all-reduce(f32[4096]{0:T(1024)S(1)} %get-tuple-element.209), channel_id=2, replica_groups=mesh['row'=16,'col'=16] {'col'}, use_global_device_ids=true, to_apply=%region_5.0.clone | all-reduce | flops 4096 | bytes 32768
  223.8 30.7 %all_gather.11 = bf16[96,4096]{1,0:T(8,128)(2,1)S(1)} all-gather(bf16[96,256]{1,0:T(8,128)(2,1)S(1)} %multiply_convert_fusion), channel_id=1, replica_groups=mesh['row'=16,'col'=16] {'row'}, dimensions={1}, use_global_device_ids=true | all-gather | bytes 835584 | tf_op jit(solution)/shard_map/all_gather | solution.py:82
  254.5 38.2 %while.31 = (s32[]{:T(128)}, f32[96,4096]{1,0:T(8,128)S(1)}, bf16[96,4096]{1,0:T(8,128)(2,1)S(1)}, bf16[4096,4096]{1,0:T(8,128)(2,1)}, s32[]{:T(128)}, /*index=5*/s32[]{:T(128)}, s32[]{:T(128)}, s32[]{:T(128)}) while((s32[]{:T(128)}, f32[96,4096]{1,0:T(8,128)S(1)}, bf16[96,4096]{1,0:T(8,128)(2,1)S(1)}, ...), condition=%wide.region_7.0_spmd.clone, body=%wide.region_6.0_spmd.clone.sunk | while | flops 202113024 | bytes 5293708 | solution.py:58
  254.5 2.3 convolution_add_fusion.2
  256.9 2.4 convolution_add_fusion.2
  259.3 2.4 convolution_add_fusion.2
  261.7 2.4 convolution_add_fusion.2
  264.0 2.4 convolution_add_fusion.2
  266.4 2.4 convolution_add_fusion.2
  268.8 2.4 convolution_add_fusion.2
  271.2 2.4 convolution_add_fusion.2
  273.6 2.4 convolution_add_fusion.2
  276.0 2.4 convolution_add_fusion.2
  278.4 2.4 convolution_add_fusion.2
  280.8 2.4 convolution_add_fusion.2
  283.1 2.4 convolution_add_fusion.2
  285.5 2.4 convolution_add_fusion.2
  287.9 2.4 convolution_add_fusion.2
  290.3 2.4 convolution_add_fusion.2
  292.7 1.1 copy-done
  294.8 69.3 %reduce-scatter.2.cloned.1.call-done = f32[96,256]{1,0:T(8,128)} async-done(((f32[96,4096]{1,0:T(8,128)}), f32[96,256]{1,0:T(8,128)}) %reduce-scatter.2.cloned.1.call-update) | async-done | bytes 98320 | tf_op jit(solution)/shard_map/reduce_scatter | solution.py:84
  364.1 0.9 broadcast_multiply_fusion
  365.9 246.6 %all-reduce.4.cloned.1.call-done = (f32[96,96]{0,1:T(8,128)}, f32[96,96]{0,1:T(8,128)}) async-done(((f32[96,96]{0,1:T(8,128)}, f32[96,96]{0,1:T(8,128)}), (f32[96,96]{0,1:T(8,128)}, f32[96,96]{0,1:T(8,128)})) %all-reduce.4.cloned.1.call-update) | async-done | bytes 73744 | tf_op jit(solution)/shard_map/psum | solution.py:102
  614.1 2.9 cholesky.44
  618.4 2.4 custom-call.13
  622.3 74.3 %psum.23 = f32[32,32]{0,1:T(8,128)S(1)} all-reduce(f32[32,32]{0,1:T(8,128)S(1)} %fusion.24), channel_id=1, replica_groups=mesh['row'=16,'col'=16] {'row','col'}, use_global_device_ids=true, to_apply=%region_13.15 | all-reduce | flops 1024 | bytes 8192 | tf_op jit(solution)/shard_map/psum | solution.py:115
  696.7 2.9 cholesky.55
  701.0 2.4 custom-call.14
  (72 shorter events, 10.6 us)
Async XLA Ops:
  7.2 356.9 %reduce-scatter.2.cloned.1.call-start = ((), (), s32[]{:S(2)}) async-start(), calls=%async_computation.1 | async-start | bytes 1671168 | tf_op jit(solution)/shard_map/reduce_scatter | solution.py:84
  65.6 156.9 %copy-start.3 = (u32[256]{0:T(256)S(1)}, u32[256]{0:T(256)}, u32[]{:S(2)}) copy-start(u32[256]{0:T(256)} %constant.134) | copy-start | bytes 3076
  65.6 158.2 %copy-start.1 = (f32[96,256]{1,0:T(8,128)S(1)}, f32[96,256]{1,0:T(8,128)}, u32[]{:S(2)}) copy-start(f32[96,256]{1,0:T(8,128)} %param.8) | copy-start | bytes 294916
  292.7 1.2 copy-start
  293.9 318.6 %all-reduce.4.cloned.1.call-start = ((), (), s32[]{:S(2)}) async-start(), calls=%async_computation.2 | async-start | bytes 196608 | tf_op jit(solution)/shard_map/psum | solution.py:102
  365.0 339.3 %copy-start.2 = (f32[96,256]{1,0:T(8,128)}, f32[96,256]{1,0:T(8,128)S(1)}, u32[]{:S(2)}) copy-start(f32[96,256]{1,0:T(8,128)S(1)} %broadcast_multiply_fusion) | copy-start | bytes 294916
Sparse Core Ops, SparseCore 0:
  294.0 70.0 reduce-scatter.1
  370.3 242.1 all-reduce.3
where the time goes:
time: 712 us; the launch traced here: 711 us
  waiting for transfers between devices  316 us (44%)
  blocking collectives  210 us (29%)
  matrix products  115 us (16%)
  local copies, waits for them, and re-layouts  39.2 us (6%)
  other arithmetic  15.3 us (2%)
  between operations  14.8 us (2%)
    psum x1, waiting for transfers between devices, per_device(): sum_a, sum_b = lax.psum((local_a, local_b), ('row', 'col'))  247 us
    psum x1, blocking collectives, per_device(): residual_gram = lax.psum(local_r, ('row', 'col')) / point_count  74.3 us
    dot_general x16, matrix products, pair_tile(): lax.dot_general(source_points, target_points, (((0,), (0,)), ((), ())), p...  73.7 us
    reduce_scatter x1, waiting for transfers between devices, per_device(): lax.psum_scatter(totals, 'col', scatter_dimension=1, tiled=True)  69.3 us
    unnamed x1, blocking collectives  58.1 us
    dot_general x16, matrix products, accumulate_add_block(): jnp.dot(columns, tile_rows, preferred_element_type=jnp.float32)  37.7 us
    all_gather x1, blocking collectives, per_device(): lax.all_gather(scaled, 'row', axis=1, tiled=True)  30.7 us
    all_gather x1, blocking collectives, per_device(): source_points = lax.all_gather(points, 'row', axis=1, tiled=True)  27.3 us
  transfers between devices with their start and end apart: 2, of which 2 were waited for; matrix products, arithmetic and copies ran while one was open for 0% of the time, Pallas kernels for 0%

commit v1 on v0

--- a/solution.py
+++ b/solution.py
@@ -112,7 +112,7 @@
         precision=lax.Precision.HIGHEST,
         preferred_element_type=jnp.float32,
     )
-    residual_gram = lax.psum(local_r, ("row", "col")) / point_count
+    residual_gram = jnp.sum(lax.all_gather(local_r, ("row", "col")), axis=0) / point_count
     factor_r = jnp.linalg.cholesky(residual_gram)
     q_block = jax.scipy.linalg.solve_triangular(factor_r, residual, lower=True)
     return (applied, gram_a, gram_b, q_block)

time: 712 us -> 751 us (1.055)
  waiting for transfers between devices: 316 us -> 427 us
  blocking collectives: 210 us -> 136 us
    all_gather x0 -> x1, waiting for transfers between devices: none -> 111 us  [per_device(): lax.all_gather(local_r, ('row', 'col'))]
    psum x1 -> x0, blocking collectives: 74.3 us -> none  [per_device(): residual_gram = lax.psum(local_r, ('row', 'col')) / point_count]
  transfers between devices with their start and end apart: 2 -> 3, of which waited for: 2 -> 3; matrix products, arithmetic and copies ran while one was open for 0% -> 0% of each run, Pallas kernels for 0% -> 0%
where the time goes in v1:
time: 751 us; the launch traced here: 750 us
  waiting for transfers between devices  427 us (57%)
  blocking collectives  136 us (18%)
  matrix products  115 us (15%)
  local copies, waits for them, and re-layouts  39.3 us (5%)
  other arithmetic  17.9 us (2%)
  between operations  14.5 us (2%)
    psum x1, waiting for transfers between devices, per_device(): sum_a, sum_b = lax.psum((local_a, local_b), ('row', 'col'))  247 us
    all_gather x1, waiting for transfers between devices, per_device(): lax.all_gather(local_r, ('row', 'col'))  111 us
    dot_general x16, matrix products, pair_tile(): lax.dot_general(source_points, target_points, (((0,), (0,)), ((), ())), p...  73.7 us
    reduce_scatter x1, waiting for transfers between devices, per_device(): lax.psum_scatter(totals, 'col', scatter_dimension=1, tiled=True)  69.3 us
    unnamed x1, blocking collectives  58.1 us
    dot_general x16, matrix products, accumulate_add_block(): jnp.dot(columns, tile_rows, preferred_element_type=jnp.float32)  37.7 us
    all_gather x1, blocking collectives, per_device(): lax.all_gather(scaled, 'row', axis=1, tiled=True)  30.7 us
    all_gather x1, blocking collectives, per_device(): source_points = lax.all_gather(points, 'row', axis=1, tiled=True)  27.3 us
  transfers between devices with their start and end apart: 3, of which 3 were waited for; matrix products, arithmetic and copies ran while one was open for 0% of the time, Pallas kernels for 0%

profile of v1, /device:TPU:1, one launch (start us, length us, event | category | flops | bytes accessed | tf_op | source)
XLA Modules:
  0.0 750.3 jit_solution(5840290401111498680)
XLA Ops:
  7.2 20.0 %all_gather.16 = f32[32,4096]{1,0:T(8,128)S(1)} all-gather(f32[32,256]{1,0:T(8,128)} %param.7), channel_id=1, replica_groups=mesh['row'=16,'col'=16] {'col'}, dimensions={1}, use_global_device_ids=true | all-gather | bytes 557056 | tf_op jit(solution)/shard_map/all_gather | solution.py:75
  27.2 27.3 %all_gather.15 = f32[32,4096]{1,0:T(8,128)S(1)} all-gather(f32[32,256]{1,0:T(8,128)} %param.7), channel_id=1, replica_groups=mesh['row'=16,'col'=16] {'row'}, dimensions={1}, use_global_device_ids=true | all-gather | bytes 557056 | tf_op jit(solution)/shard_map/all_gather | solution.py:76
  54.6 11.0 %broadcast_in_dim.20 = bf16[4096,4096]{1,0:T(8,128)(2,1)} broadcast(bf16[]{:T(256)} %constant.130.clone.1), dimensions={} | broadcast | bytes 33554432 | tf_op jit(solution)/shard_map/broadcast_in_dim | solution.py:42
  65.6 98.8 %while.30 = (s32[]{:T(128)}, f32[4096]{0:T(1024)S(1)}, bf16[4096,4096]{1,0:T(8,128)(2,1)}, f32[4096]{0:T(1024)S(1)}, f32[4096]{0:T(1024)S(1)}, /*index=5*/f32[32...) while((s32[]{:T(128)}, f32[4096]{0:T(1024)S(1)}, ...), condition=%wide.region_4.0_spmd.clone, body=%wide.region_2.0_spmd.clone.sunk | while | flops 408948736 | bytes 6933681 | solution.py:43
  65.6 4.6 fusion.40
  70.3 1.5 convert_dynamic-update-slice_fusion.2
  71.8 4.6 fusion.40
  76.5 1.4 convert_dynamic-update-slice_fusion.2
  78.0 4.6 fusion.40
  82.6 1.5 convert_dynamic-update-slice_fusion.2
  84.1 4.6 fusion.40
  88.7 1.5 convert_dynamic-update-slice_fusion.2
  90.3 4.6 fusion.40
  94.9 1.5 convert_dynamic-update-slice_fusion.2
  96.5 4.6 fusion.40
  101.2 1.4 convert_dynamic-update-slice_fusion.2
  102.7 4.6 fusion.40
  107.3 1.5 convert_dynamic-update-slice_fusion.2
  108.9 4.6 fusion.40
  113.5 1.5 convert_dynamic-update-slice_fusion.2
  115.0 4.6 fusion.40
  119.7 1.5 convert_dynamic-update-slice_fusion.2
  121.2 4.6 fusion.40
  125.8 1.4 convert_dynamic-update-slice_fusion.2
  127.4 4.6 fusion.40
  132.0 1.5 convert_dynamic-update-slice_fusion.2
  133.5 4.6 fusion.40
  138.1 1.5 convert_dynamic-update-slice_fusion.2
  139.7 4.6 fusion.40
  144.3 1.5 convert_dynamic-update-slice_fusion.2
  145.9 4.6 fusion.40
  150.5 1.4 convert_dynamic-update-slice_fusion.2
  152.1 4.6 fusion.40
  156.7 1.5 convert_dynamic-update-slice_fusion.2
  158.3 4.6 fusion.40
  162.9 1.5 convert_dynamic-update-slice_fusion.2
  164.3 58.1 %all-reduce = f32[4096]{0:T(1024)S(1)} all-reduce(f32[4096]{0:T(1024)S(1)} %get-tuple-element.209), channel_id=3, replica_groups=mesh['row'=16,'col'=16] {'col'}, use_global_device_ids=true, to_apply=%region_5.0.clone | all-reduce | flops 4096 | bytes 32768
  223.8 30.7 %all_gather.17 = bf16[96,4096]{1,0:T(8,128)(2,1)S(1)} all-gather(bf16[96,256]{1,0:T(8,128)(2,1)S(1)} %multiply_convert_fusion), channel_id=1, replica_groups=mesh['row'=16,'col'=16] {'row'}, dimensions={1}, use_global_device_ids=true | all-gather | bytes 835584 | tf_op jit(solution)/shard_map/all_gather | solution.py:82
  254.5 38.2 %while.31 = (s32[]{:T(128)}, f32[96,4096]{1,0:T(8,128)S(1)}, bf16[96,4096]{1,0:T(8,128)(2,1)S(1)}, bf16[4096,4096]{1,0:T(8,128)(2,1)}, s32[]{:T(128)}, /*index=5*/s32[]{:T(128)}, s32[]{:T(128)}, s32[]{:T(128)}) while((s32[]{:T(128)}, f32[96,4096]{1,0:T(8,128)S(1)}, bf16[96,4096]{1,0:T(8,128)(2,1)S(1)}, ...), condition=%wide.region_7.0_spmd.clone, body=%wide.region_6.0_spmd.clone.sunk | while | flops 202113024 | bytes 5293708 | solution.py:58
  254.5 2.3 convolution_add_fusion.2
  256.9 2.4 convolution_add_fusion.2
  259.3 2.4 convolution_add_fusion.2
  261.7 2.4 convolution_add_fusion.2
  264.0 2.4 convolution_add_fusion.2
  266.4 2.4 convolution_add_fusion.2
  268.8 2.4 convolution_add_fusion.2
  271.2 2.4 convolution_add_fusion.2
  273.6 2.4 convolution_add_fusion.2
  276.0 2.4 convolution_add_fusion.2
  278.4 2.4 convolution_add_fusion.2
  280.8 2.4 convolution_add_fusion.2
  283.1 2.4 convolution_add_fusion.2
  285.5 2.4 convolution_add_fusion.2
  287.9 2.4 convolution_add_fusion.2
  290.3 2.4 convolution_add_fusion.2
  292.7 1.1 copy-done
  294.8 69.3 %reduce-scatter.2.cloned.1.call-done = f32[96,256]{1,0:T(8,128)} async-done(((f32[96,4096]{1,0:T(8,128)}), f32[96,256]{1,0:T(8,128)}) %reduce-scatter.2.cloned.1.call-update) | async-done | bytes 98320 | tf_op jit(solution)/shard_map/reduce_scatter | solution.py:84
  365.9 246.6 %all-reduce.4.cloned.1.call-done = (f32[96,96]{0,1:T(8,128)}, f32[96,96]{0,1:T(8,128)}) async-done(((f32[96,96]{0,1:T(8,128)}, f32[96,96]{0,1:T(8,128)}), (f32[96,96]{0,1:T(8,128)}, f32[96,96]{0,1:T(8,128)})) %all-reduce.4.cloned.1.call-update) | async-done | bytes 73744 | tf_op jit(solution)/shard_map/psum | solution.py:102
  613.4 2.9 cholesky.44
  617.7 2.4 custom-call.13
  622.9 110.6 %all-gather.3.cloned.1.call-done = f32[8192,32]{1,0:T(8,128)} async-done(((f32[32,32]{1,0:T(8,128)}), f32[8192,32]{1,0:T(8,128)}) %all-gather.3.cloned.1.call-update) | async-done | bytes 1048592 | tf_op jit(solution)/shard_map/all_gather | solution.py:115
  733.6 2.5 reduce_sum.42
  736.3 2.9 cholesky.55
  740.5 2.4 custom-call.14
  (76 shorter events, 12.3 us)
Async XLA Ops:
  7.2 356.9 %reduce-scatter.2.cloned.1.call-start = ((), (), s32[]{:S(2)}) async-start(), calls=%async_computation.1 | async-start | bytes 1671168 | tf_op jit(solution)/shard_map/reduce_scatter | solution.py:84
  65.6 156.9 %copy-start.3 = (u32[256]{0:T(256)S(1)}, u32[256]{0:T(256)}, u32[]{:S(2)}) copy-start(u32[256]{0:T(256)} %constant.134) | copy-start | bytes 3076
  65.6 158.2 %copy-start.1 = (f32[96,256]{1,0:T(8,128)S(1)}, f32[96,256]{1,0:T(8,128)}, u32[]{:S(2)}) copy-start(f32[96,256]{1,0:T(8,128)} %param.8) | copy-start | bytes 294916
  292.7 1.2 copy-start
  293.9 318.6 %all-reduce.4.cloned.1.call-start = ((), (), s32[]{:S(2)}) async-start(), calls=%async_computation.3 | async-start | bytes 196608 | tf_op jit(solution)/shard_map/psum | solution.py:102
  365.0 378.8 %copy-start.2 = (f32[96,256]{1,0:T(8,128)}, f32[96,256]{1,0:T(8,128)S(1)}, u32[]{:S(2)}) copy-start(f32[96,256]{1,0:T(8,128)S(1)} %broadcast_multiply_fusion) | copy-start | bytes 294916
  365.9 367.7 %all-gather.3.cloned.1.call-start = ((), (), s32[]{:S(2)}) async-start(), calls=%async_computation.2 | async-start | bytes 4210688 | tf_op jit(solution)/shard_map/all_gather | solution.py:115
Sparse Core Ops, SparseCore 0:
  294.0 70.0 reduce-scatter.1
  370.3 242.1 all-reduce.3
  621.6 111.8 all-gather.2
